TPU v7x, 512 devices: a whole 4x4x16 slice. The times are simulated.
512 devices in a mesh: gx: 128 (over y_hi, z, x), trait: 4 (over y_lo, core).
Axes of the slice: x: 4, y: 4 (y_hi: 2, y_lo: 2; y = y_hi * 2 + y_lo), z: 16, core: 2. Of those that a mesh axis runs over, the one named last changes fastest.
Arguments:
- initial: float32 [1024, 128, 1024], P('gx', None, 'trait'), may hold values from 0.2 to 2
- section_one: float32 [1024, 128, 1024], P('gx', None, 'trait'), may hold values from 0.2 to 2
- section_two: float32 [1024, 128, 1024], P('gx', None, 'trait'), may hold values from 0.2 to 2
- kernels: bfloat16 [2, 1024, 1024], P(None, None, 'trait'), may hold values from -0.1875 to 0.1875
- growth: float32 [1024], P('trait'), may hold values from -3 to 3
- death_rate: float32 [1024], P('trait'), may hold values from 0.5 to 8
Outputs:
- new_one: float32 [1024, 128, 1024], P('gx', None, 'trait')
- new_two: float32 [1024, 128, 1024], P('gx', None, 'trait')
All inputs are finite; a program needn't handle non-finite values.
Results may differ from a plain program's by a relative error of at most 0.002.
Values may be sent and summed in bfloat16 or wider, within the bound.
A program may use at most 64 MiB of HBM per device.

v0:
```python
import jax
import jax.numpy as jnp
from jax import lax
from jax.sharding import PartitionSpec as P

DIFFUSION = 0.25
STEP_SIZE = 0.5


def with_halo(cells, sides, width):
    for axis, dim in sides:
        count = lax.axis_size(axis)
        head = lax.slice_in_dim(cells, 0, width, axis=dim)
        tail = lax.slice_in_dim(cells, cells.shape[dim] - width, cells.shape[dim], axis=dim)
        cells = jnp.concatenate(
            [
                lax.ppermute(tail, axis, [(i, (i + 1) % count) for i in range(count)]),
                cells,
                lax.ppermute(head, axis, [((i + 1) % count, i) for i in range(count)]),
            ],
            axis=dim,
        )
    return cells


def local(initial, section_one, section_two, kernels, growth, death_rate):
    first_dt = STEP_SIZE / 3.0
    second_dt = 2.0 * STEP_SIZE / 3.0

    def products(core):
        xcount, ycount, owned = core.shape
        flat = core.astype(jnp.bfloat16).reshape(xcount * ycount, owned)
        piece = lax.all_gather(flat, "trait", axis=1, tiled=True)
        compete = jnp.dot(piece, kernels[0], preferred_element_type=jnp.float32)
        mutate = jnp.dot(piece, kernels[1], preferred_element_type=jnp.float32)
        compete = compete.astype(jnp.bfloat16)
        mutate = mutate.astype(jnp.bfloat16)
        return (
            compete.astype(jnp.float32).reshape(xcount, ycount, owned),
            mutate.astype(jnp.float32).reshape(xcount, ycount, owned),
        )

    def explicit(padded):
        core = padded[1:-1]
        lapl = padded[2:] + padded[:-2] + jnp.roll(core, 1, 1) + jnp.roll(core, -1, 1) - 4.0 * core
        compete, mutate = products(core)
        return DIFFUSION * lapl + core * (growth - compete) + mutate - core

    padded_pair = with_halo(jnp.stack([section_one, section_two]), (("gx", 1),), 1)
    expl_one = explicit(padded_pair[0])
    expl_two = explicit(padded_pair[1])
    full_one = expl_one - death_rate * section_one
    full_two = expl_two - death_rate * section_two
    result = (
        initial
        + first_dt * death_rate * section_one
        + STEP_SIZE * (5.0 / 12.0 * full_one - 1.0 / 12.0 * full_two)
    ) / (1.0 + first_dt * death_rate)
    new_one, full_one, full_two = (result, full_one, full_two)
    padded_new = with_halo(new_one, (("gx", 0),), 1)
    expl_new = explicit(padded_new)
    new_two = (
        new_one
        + second_dt * (expl_new - expl_one)
        + second_dt * death_rate * section_two
        + STEP_SIZE / 3.0 * (full_one + full_two)
    ) / (1.0 + second_dt * death_rate)
    return (new_one, new_two)


def solution(mesh):
    in_specs = (
        P("gx", None, "trait"),
        P("gx", None, "trait"),
        P("gx", None, "trait"),
        P(None, None, "trait"),
        P("trait"),
        P("trait"),
    )
    out_specs = (P("gx", None, "trait"), P("gx", None, "trait"))
    return jax.shard_map(local, mesh=mesh, in_specs=in_specs, out_specs=out_specs, check_vma=False)
```

profile of v0, /device:TPU:1, one launch (start us, length us, event | category | flops | bytes accessed | tf_op | source)
XLA Modules:
  0.0 153.2 jit_solution(10018028069680694838)
XLA Ops:
  7.2 2.2 %convert_element_type.41 = bf16[8,128,256]{2,1,0:T(8,128)(2,1)} convert(f32[8,128,256]{2,1,0:T(8,128)} %param.7) | non-fusion elementwise | flops 262144 | bytes 1572864 | tf_op jit(solution)/shard_map/convert_element_type | solution.py:32
  9.5 0.8 convert_element_type.45
  10.5 16.8 %collective-permute-start = (f32[2,1,128,256]{3,2,1,0:T(8,128)S(1)}, f32[2,1,128,256]{3,2,1,0:T(8,128)S(1)}, u32[]{:S(2)}, u32[]{:S(2)}) collective-permute-start(f32[2,1,128,256]{3,2,1,0:T(8,128)S(1)} %get-tuple-element.6), channel_id=1, source_target_pairs={{4,0},{8,4},{12,8},{16,12},{20,16},{24,20},{28,24},{32,28},{36,32}... | collective-permute-start | bytes 786440 | tf_op jit(solution)/shard_map/ppermute | solution.py:19
  27.3 1.9 %collective-permute-start.1 = (f32[2,1,128,256]{3,2,1,0:T(8,128)S(1)}, f32[2,1,128,256]{3,2,1,0:T(8,128)S(1)}, u32[]{:S(2)}, u32[]{:S(2)}) collective-permute-start(f32[2,1,128,256]{3,2,1,0:T(8,128)S(1)} %get-tuple-element.7), channel_id=1, source_target_pairs={{0,4},{4,8},{8,12},{12,16},{16,20},{20,24},{24,28},{28,32},{32,36}... | collective-permute-start | bytes 786440 | tf_op jit(solution)/shard_map/ppermute | solution.py:17
  29.2 0.6 broadcast_multiply_fusion
  29.9 2.2 %fusion.54 = (f32[8,127,256]{2,1,0:T(8,128)}, f32[8,127,256]{2,1,0:T(8,128)}, f32[8,127,256]{2,1,0:T(8,128)}, f32[8,127,256]{2,1,0:T(8,128)}) fusion(f32[8,128,256]{2,1,0:T(8,128)S(1)} %copy-done.1, f32[8,128,256]{2,1,0:T(8,128)S(1)} %copy-done), kind=kLoop, calls=%fused_computation.76 | loop fusion | bytes 8323072 | tf_op jit(solution)/shard_map/jit(_roll_static)/slice | solution.py:45
  32.0 26.1 %all-gather.4.cloned.1.call-done = bf16[1024,1024]{1,0:T(8,128)(2,1)} async-done(((bf16[1024,256]{1,0:T(8,128)(2,1)}), bf16[1024,1024]{1,0:T(8,128)(2,1)}) %all-gather.4.cloned.1.call-update) | async-done | bytes 2097168 | tf_op jit(solution)/shard_map/all_gather | solution.py:33
  58.2 3.3 %convolution_convert_fusion.4 = bf16[1024,256]{1,0:T(8,128)(2,1)} fusion(bf16[1024,1024]{1,0:T(8,128)(2,1)} %all-gather.4.cloned.1.call-done, bf16[2,1024,256]{2,1,0:T(8,128)(2,1)} %param.9), kind=kOutput, calls=%fused_computation.4 | convolution fusion | flops 537133056 | bytes 3145728 | tf_op jit(solution)/shard_map/dot_general | solution.py:35
  61.5 1.5 convolution_convert_fusion.5
  63.0 29.3 %all-gather.6.cloned.1.call-done = bf16[1024,1024]{1,0:T(8,128)(2,1)} async-done(((bf16[1024,256]{1,0:T(8,128)(2,1)}), bf16[1024,1024]{1,0:T(8,128)(2,1)}) %all-gather.6.cloned.1.call-update) | async-done | bytes 2097168 | tf_op jit(solution)/shard_map/all_gather | solution.py:33
  92.3 2.5 %convolution_convert_fusion.2 = bf16[1024,256]{1,0:T(8,128)(2,1)S(1)} fusion(bf16[1024,1024]{1,0:T(8,128)(2,1)} %all-gather.6.cloned.1.call-done, bf16[2,1024,256]{2,1,0:T(8,128)(2,1)} %param.9), kind=kOutput, calls=%fused_computation.2 | convolution fusion | flops 537133056 | bytes 3145728 | tf_op jit(solution)/shard_map/dot_general | solution.py:35
  95.0 0.7 convolution_convert_fusion.3
  95.8 0.7 copy-done.14
  96.5 0.4 copy-done.9
  97.8 3.5 %fusion.47 = (bf16[8,128,256]{2,1,0:T(8,128)(2,1)}, f32[8,128,256]{2,1,0:T(8,128)S(1)}, f32[8,128,256]{2,1,0:T(8,128)}, f32[8,128,256]{2,1,0:T(8,128)}) fusion(f32[256]{0:T(256)S(1)} %get-tuple-element.23, f32[8,128,256]{2,1,0:T(8,128)S(1)} %copy-done, f32[256]{0:T(256)S(1)} %copy-done.15, f32[8,128,256]{2,1,0:T(8,128)S(1)} %copy-done.11, ...), kind=kLoop, calls=%fused_computation.71 | loop fusion | flops 13369344 | bytes 15732736 | tf_op jit(solution)/shard_map/convert_element_type | solution.py:32
  101.4 0.7 fusion.52
  102.1 9.9 %collective-permute-start.2 = (f32[1,128,256]{2,1,0:T(8,128)}, f32[1,128,256]{2,1,0:T(8,128)S(1)}, u32[]{:S(2)}, u32[]{:S(2)}) collective-permute-start(f32[1,128,256]{2,1,0:T(8,128)} %get-tuple-element.12), channel_id=1, source_target_pairs={{4,0},{8,4},{12,8},{16,12},{20,16},{24,20},{28,24},{32,28},{36,32}... | collective-permute-start | bytes 393224 | tf_op jit(solution)/shard_map/ppermute | solution.py:19
  112.1 1.9 %collective-permute-start.3 = (f32[1,128,256]{2,1,0:T(8,128)S(1)}, f32[1,128,256]{2,1,0:T(8,128)S(1)}, u32[]{:S(2)}, u32[]{:S(2)}) collective-permute-start(f32[1,128,256]{2,1,0:T(8,128)S(1)} %get-tuple-element.13), channel_id=1, source_target_pairs={{0,4},{4,8},{8,12},{12,16},{16,20},{20,24},{24,28},{28,32},{32,36}... | collective-permute-start | bytes 393224 | tf_op jit(solution)/shard_map/ppermute | solution.py:17
  114.0 1.5 fusion.50
  115.5 24.3 %all-gather.8.cloned.1.call-done = bf16[1024,1024]{1,0:T(8,128)(2,1)} async-done(((bf16[1024,256]{1,0:T(8,128)(2,1)}), bf16[1024,1024]{1,0:T(8,128)(2,1)}) %all-gather.8.cloned.1.call-update) | async-done | bytes 2097168 | tf_op jit(solution)/shard_map/all_gather | solution.py:33
  139.8 2.5 %convolution_convert_fusion = bf16[1024,256]{1,0:T(8,128)(2,1)S(1)} fusion(bf16[1024,1024]{1,0:T(8,128)(2,1)} %all-gather.8.cloned.1.call-done, bf16[2,1024,256]{2,1,0:T(8,128)(2,1)} %param.9), kind=kOutput, calls=%fused_computation | convolution fusion | flops 537133056 | bytes 3145728 | tf_op jit(solution)/shard_map/dot_general | solution.py:35
  142.5 0.7 convolution_convert_fusion.1
  143.3 0.4 copy-done.3
  144.7 2.0 %fusion.13 = f32[8,128,256]{2,1,0:T(8,128)} fusion(f32[8,128,256]{2,1,0:T(8,128)S(1)} %get-tuple-element.3, f32[8,128,256]{2,1,0:T(8,128)S(1)} %copy-done.3, f32[1,128,256]{2,1,0:T(8,128)S(1)} %collective-permute-done.3, f32[1,128,256]{2,1,0:T(8,128)S(1)} %collective-permute-done.2, f32[8,127,256]{2,1,0:T(8,128)S(1)} %copy-done.6, ...), kind=kLoop, calls=%fused_computation.20 | loop fusion | flops 7340032 | bytes 9703424 | tf_op jit(solution)/shard_map/div | solution.py:62
  (64 shorter events, 2.4 us)
Async XLA Ops:
  7.2 3.3 %copy-start = (f32[8,128,256]{2,1,0:T(8,128)S(1)}, f32[8,128,256]{2,1,0:T(8,128)}, u32[]{:S(2)}) copy-start(f32[8,128,256]{2,1,0:T(8,128)} %param.7) | copy-start | bytes 3145732
  7.2 2.4 %copy-start.1 = (f32[8,128,256]{2,1,0:T(8,128)S(1)}, f32[8,128,256]{2,1,0:T(8,128)}, u32[]{:S(2)}) copy-start(f32[8,128,256]{2,1,0:T(8,128)} %param.8) | copy-start | bytes 3145732
  7.2 51.0 %all-gather.4.cloned.1.call-start = ((), (), s32[]{:S(2)}) async-start(), calls=%async_computation | async-start | bytes 2621440 | tf_op jit(solution)/shard_map/all_gather | solution.py:33
  9.5 19.8 %copy-start.15 = (f32[256]{0:T(256)S(1)}, f32[256]{0:T(256)}, u32[]{:S(2)}) copy-start(f32[256]{0:T(256)} %param.11) | copy-start | bytes 3076
  9.5 82.8 %all-gather.6.cloned.1.call-start = ((), (), s32[]{:S(2)}) async-start(), calls=%async_computation.1 | async-start | bytes 2621440 | tf_op jit(solution)/shard_map/all_gather | solution.py:33
  10.4 129.4 %all-gather.8.cloned.1.call-start = ((), (), s32[]{:S(2)}) async-start(), calls=%async_computation.2 | async-start | bytes 2621440 | tf_op jit(solution)/shard_map/all_gather | solution.py:33
  10.5 85.2 %collective-permute-start = (f32[2,1,128,256]{3,2,1,0:T(8,128)S(1)}, f32[2,1,128,256]{3,2,1,0:T(8,128)S(1)}, u32[]{:S(2)}, u32[]{:S(2)}) collective-permute-start(f32[2,1,128,256]{3,2,1,0:T(8,128)S(1)} %get-tuple-element.6), channel_id=1, source_target_pairs={{4,0},{8,4},{12,8},{16,12},{20,16},{24,20},{28,24},{32,28},{36,32}... | collective-permute-start | bytes 786440 | tf_op jit(solution)/shard_map/ppermute | solution.py:19
  27.3 68.4 %collective-permute-start.1 = (f32[2,1,128,256]{3,2,1,0:T(8,128)S(1)}, f32[2,1,128,256]{3,2,1,0:T(8,128)S(1)}, u32[]{:S(2)}, u32[]{:S(2)}) collective-permute-start(f32[2,1,128,256]{3,2,1,0:T(8,128)S(1)} %get-tuple-element.7), channel_id=1, source_target_pairs={{0,4},{4,8},{8,12},{12,16},{16,20},{20,24},{24,28},{28,32},{32,36}... | collective-permute-start | bytes 786440 | tf_op jit(solution)/shard_map/ppermute | solution.py:17
  58.2 3.3 %copy-start.21 = (bf16[1024,1024]{1,0:T(8,128)(2,1)S(1)}, bf16[1024,1024]{1,0:T(8,128)(2,1)}, u32[]{:S(2)}) copy-start(bf16[1024,1024]{1,0:T(8,128)(2,1)} %all-gather.4.cloned.1.call-done) | copy-start | bytes 6291460
  58.2 3.3 %copy-start.24 = (bf16[2,1024,256]{2,1,0:T(8,128)(2,1)S(1)}, bf16[2,1024,256]{2,1,0:T(8,128)(2,1)}, u32[]{:S(2)}) copy-start(bf16[2,1024,256]{2,1,0:T(8,128)(2,1)} %param.9) | copy-start | bytes 3145732
  92.3 2.5 %copy-start.22 = (bf16[1024,1024]{1,0:T(8,128)(2,1)S(1)}, bf16[1024,1024]{1,0:T(8,128)(2,1)}, u32[]{:S(2)}) copy-start(bf16[1024,1024]{1,0:T(8,128)(2,1)} %all-gather.6.cloned.1.call-done) | copy-start | bytes 6291460
  92.3 2.6 %copy-start.25 = (bf16[2,1024,256]{2,1,0:T(8,128)(2,1)S(1)}, bf16[2,1024,256]{2,1,0:T(8,128)(2,1)}, u32[]{:S(2)}) copy-start(bf16[2,1024,256]{2,1,0:T(8,128)(2,1)} %param.9) | copy-start | bytes 3145732
  95.0 2.3 %copy-start.10 = (f32[8,127,256]{2,1,0:T(8,128)S(1)}, f32[8,127,256]{2,1,0:T(8,128)}, u32[]{:S(2)}) copy-start(f32[8,127,256]{2,1,0:T(8,128)} %get-tuple-element.29) | copy-start | bytes 3121156
  95.0 2.6 %copy-start.11 = (f32[8,128,256]{2,1,0:T(8,128)S(1)}, f32[8,128,256]{2,1,0:T(8,128)}, u32[]{:S(2)}) copy-start(f32[8,128,256]{2,1,0:T(8,128)} %param.6) | copy-start | bytes 3145732
  95.0 2.7 %copy-start.12 = (bf16[1024,256]{1,0:T(8,128)(2,1)S(1)}, bf16[1024,256]{1,0:T(8,128)(2,1)}, u32[]{:S(2)}) copy-start(bf16[1024,256]{1,0:T(8,128)(2,1)} %convolution_convert_fusion.4) | copy-start | bytes 1572868
  95.0 2.8 %copy-start.13 = (bf16[1024,256]{1,0:T(8,128)(2,1)S(1)}, bf16[1024,256]{1,0:T(8,128)(2,1)}, u32[]{:S(2)}) copy-start(bf16[1024,256]{1,0:T(8,128)(2,1)} %convolution_convert_fusion.5) | copy-start | bytes 1572868
  95.0 2.8 %copy-start.17 = (f32[256]{0:T(256)S(1)}, f32[256]{0:T(256)}, u32[]{:S(2)}) copy-start(f32[256]{0:T(256)} %param.10) | copy-start | bytes 3076
  101.4 41.9 %copy-start.2 = (f32[8,128,256]{2,1,0:T(8,128)}, f32[8,128,256]{2,1,0:T(8,128)S(1)}, u32[]{:S(2)}) copy-start(f32[8,128,256]{2,1,0:T(8,128)S(1)} %get-tuple-element.3) | copy-start | bytes 3145732
  102.1 41.1 %collective-permute-start.2 = (f32[1,128,256]{2,1,0:T(8,128)}, f32[1,128,256]{2,1,0:T(8,128)S(1)}, u32[]{:S(2)}, u32[]{:S(2)}) collective-permute-start(f32[1,128,256]{2,1,0:T(8,128)} %get-tuple-element.12), channel_id=1, source_target_pairs={{4,0},{8,4},{12,8},{16,12},{20,16},{24,20},{28,24},{32,28},{36,32}... | collective-permute-start | bytes 393224 | tf_op jit(solution)/shard_map/ppermute | solution.py:19
  112.1 31.2 %collective-permute-start.3 = (f32[1,128,256]{2,1,0:T(8,128)S(1)}, f32[1,128,256]{2,1,0:T(8,128)S(1)}, u32[]{:S(2)}, u32[]{:S(2)}) collective-permute-start(f32[1,128,256]{2,1,0:T(8,128)S(1)} %get-tuple-element.13), channel_id=1, source_target_pairs={{0,4},{4,8},{8,12},{12,16},{16,20},{20,24},{24,28},{28,32},{32,36}... | collective-permute-start | bytes 393224 | tf_op jit(solution)/shard_map/ppermute | solution.py:17
  139.8 2.5 %copy-start.23 = (bf16[1024,1024]{1,0:T(8,128)(2,1)S(1)}, bf16[1024,1024]{1,0:T(8,128)(2,1)}, u32[]{:S(2)}) copy-start(bf16[1024,1024]{1,0:T(8,128)(2,1)} %all-gather.8.cloned.1.call-done) | copy-start | bytes 6291460
  139.8 2.6 %copy-start.26 = (bf16[2,1024,256]{2,1,0:T(8,128)(2,1)S(1)}, bf16[2,1024,256]{2,1,0:T(8,128)(2,1)}, u32[]{:S(2)}) copy-start(bf16[2,1024,256]{2,1,0:T(8,128)(2,1)} %param.9) | copy-start | bytes 3145732
  142.5 2.2 %copy-start.6 = (f32[8,127,256]{2,1,0:T(8,128)S(1)}, f32[8,127,256]{2,1,0:T(8,128)}, u32[]{:S(2)}) copy-start(f32[8,127,256]{2,1,0:T(8,128)} %get-tuple-element.9) | copy-start | bytes 3121156
  142.5 2.2 %copy-start.16 = (f32[256]{0:T(256)S(1)}, f32[256]{0:T(256)}, u32[]{:S(2)}) copy-start(f32[256]{0:T(256)} %param.11) | copy-start | bytes 3076
  (10 other events, 16.8 us)
Sparse Core Ops, SparseCore 0:
  10.1 48.0 all-gather.3
  60.3 32.0 all-gather.5
  101.5 38.2 all-gather.7
where the time goes:
time: 153 us
  waiting for transfers between devices  79.8 us (52%)
  starting transfers between devices  30.7 us (20%)
  between operations  14 us (9%)
  matrix products  11.3 us (7%)
  other arithmetic  9.25 us (6%)
  local copies, waits for them, and re-layouts  8.15 us (5%)
    all_gather x3, waiting for transfers between devices, products(): piece = lax.all_gather(flat, 'trait', axis=1, tiled=True)  79.7 us
    ppermute x2, starting transfers between devices, with_halo(): lax.ppermute(head, axis, [((i + 1) % count, i) for i in range(count)])  26.7 us
    dot_general x3, matrix products, products(): mutate = jnp.dot(piece, kernels[1], preferred_element_type=jnp.float32)  8.39 us
    convert_element_type x3, other arithmetic, products(): flat = core.astype(jnp.bfloat16).reshape(xcount * ycount, owned)  6.6 us
    ppermute x2, starting transfers between devices, with_halo(): lax.ppermute(tail, axis, [(i, (i + 1) % count) for i in range(count)])  3.84 us
    unnamed x54, local copies, waits for them, and re-layouts  3.7 us
  transfers between devices with their start and end apart: 7, of which 3 were waited for; matrix products, arithmetic and copies ran while one was open for 11% of the time, Pallas kernels for 0%

commit v1 on v0

--- a/solution.py
+++ b/solution.py
@@ -5,6 +5,9 @@
 
 DIFFUSION = 0.25
 STEP_SIZE = 0.5
+link_circles = lambda my_tile, row_axis: jnp.concatenate(
+    lax.all_to_all(jnp.stack(lax.axis_size(row_axis) * [my_tile]), row_axis, 0, 0), axis=1
+)
 
 
 def with_halo(cells, sides, width):
@@ -30,7 +33,7 @@
     def products(core):
         xcount, ycount, owned = core.shape
         flat = core.astype(jnp.bfloat16).reshape(xcount * ycount, owned)
-        piece = lax.all_gather(flat, "trait", axis=1, tiled=True)
+        piece = link_circles(flat, "trait")
         compete = jnp.dot(piece, kernels[0], preferred_element_type=jnp.float32)
         mutate = jnp.dot(piece, kernels[1], preferred_element_type=jnp.float32)
         compete = compete.astype(jnp.bfloat16)

time: 153 us -> 133 us (0.87)
  waiting for transfers between devices: 79.8 us -> 46.7 us
  starting transfers between devices: 30.7 us -> 47.1 us
  between operations: 14 us -> 1 us
  local copies, waits for them, and re-layouts: 8.15 us -> 14.1 us
  matrix products: 11.3 us -> 16.4 us
  other arithmetic: 9.25 us -> 7.46 us
    all_gather x3 -> x0, waiting for transfers between devices: 79.7 us -> none  [products(): piece = lax.all_gather(flat, 'trait', axis=1, tiled=True)]
    all_to_all x0 -> x3, waiting for transfers between devices: none -> 46.7 us  [lax.all_to_all(jnp.stack(lax.axis_size(row_axis) * [my_tile]), row_axis,...]
    all_to_all x0 -> x3, starting transfers between devices: none -> 22.1 us  [lax.all_to_all(jnp.stack(lax.axis_size(row_axis) * [my_tile]), row_axis,...]
    another operation x0 -> x4, local copies, waits for them, and re-layouts: none -> 8.32 us  [jnp.stack(lax.axis_size(row_axis) * [my_tile])]
    ppermute x2, starting transfers between devices: 26.7 us -> 21.1 us  [with_halo(): lax.ppermute(head, axis, [((i + 1) % count, i) for i in range(count)])]
    dot_general x3, matrix products: 2.94 us -> 8.15 us  [products(): compete = jnp.dot(piece, kernels[0], preferred_element_type=jnp.float32)]
    unnamed x54 -> x48, local copies, waits for them, and re-layouts: 3.7 us -> 1.01 us
    convert_element_type x3, other arithmetic: 6.6 us -> 4.86 us  [products(): flat = core.astype(jnp.bfloat16).reshape(xcount * ycount, owned)]
  transfers between devices with their start and end apart: 7 -> 7, of which waited for: 3 -> 3; matrix products, arithmetic and copies ran while one was open for 11% -> 16% of each run, Pallas kernels for 0% -> 0%
where the time goes in v1:
time: 133 us
  starting transfers between devices  47.1 us (35%)
  waiting for transfers between devices  46.7 us (35%)
  matrix products  16.4 us (12%)
  local copies, waits for them, and re-layouts  14.1 us (11%)
  other arithmetic  7.46 us (6%)
    all_to_all x3, waiting for transfers between devices, lax.all_to_all(jnp.stack(lax.axis_size(row_axis) * [my_tile]), row_axis,...  46.7 us
    all_to_all x3, starting transfers between devices, lax.all_to_all(jnp.stack(lax.axis_size(row_axis) * [my_tile]), row_axis,...  22.1 us
    ppermute x2, starting transfers between devices, with_halo(): lax.ppermute(head, axis, [((i + 1) % count, i) for i in range(count)])  21.1 us
    another operation x4, local copies, waits for them, and re-layouts, jnp.stack(lax.axis_size(row_axis) * [my_tile])  8.32 us
    dot_general x3, matrix products, products(): mutate = jnp.dot(piece, kernels[1], preferred_element_type=jnp.float32)  8.23 us
    dot_general x3, matrix products, products(): compete = jnp.dot(piece, kernels[0], preferred_element_type=jnp.float32)  8.15 us
    convert_element_type x3, other arithmetic, products(): flat = core.astype(jnp.bfloat16).reshape(xcount * ycount, owned)  4.86 us
    ppermute x2, starting transfers between devices, with_halo(): lax.ppermute(tail, axis, [(i, (i + 1) % count) for i in range(count)])  3.84 us
  transfers between devices with their start and end apart: 7, of which 3 were waited for; matrix products, arithmetic and copies ran while one was open for 16% of the time, Pallas kernels for 0%

profile of v1, /device:TPU:1, one launch (start us, length us, event | category | flops | bytes accessed | tf_op | source)
XLA Modules:
  0.0 132.6 jit_solution(5568908567767292371)
XLA Ops:
  2.1 1.6 %stack.22 = bf16[4,1024,256]{1,2,0:T(8,128)(2,1)} broadcast(bf16[1024,256]{0,1:T(8,128)(2,1)S(1)} %copy.9), dimensions={1,2} | broadcast | bytes 2621440 | tf_op jit(solution)/shard_map/stack | solution.py:9
  3.7 11.4 %all-to-all-start.1 = ((bf16[4,1024,256]{1,2,0:T(8,128)(2,1)}), bf16[4,1024,256]{1,2,0:T(8,128)(2,1)}, u32[]{:S(2)}, u32[]{:S(2)}) async-start(bf16[4,1024,256]{1,2,0:T(8,128)(2,1)} %stack.22), calls=%async_computation.1 | async-start | bytes 4194304 | tf_op jit(solution)/shard_map/all_to_all | solution.py:9
  15.4 24.7 %all-to-all-done.1 = bf16[4,1024,256]{1,2,0:T(8,128)(2,1)} async-done(((bf16[4,1024,256]{1,2,0:T(8,128)(2,1)}), bf16[4,1024,256]{1,2,0:T(8,128)(2,1)}, u32[]{:S(2)}, u32[]{:S(2)}) %all-to-all-start.1) | async-done | bytes 2097184 | tf_op jit(solution)/shard_map/all_to_all | solution.py:9
  40.1 1.6 %stack.21 = bf16[4,1024,256]{1,2,0:T(8,128)(2,1)} broadcast(bf16[1024,256]{0,1:T(8,128)(2,1)S(1)} %copy.8), dimensions={1,2} | broadcast | bytes 2621440 | tf_op jit(solution)/shard_map/stack | solution.py:9
  41.7 5.4 %all-to-all-start = ((bf16[4,1024,256]{1,2,0:T(8,128)(2,1)}), bf16[4,1024,256]{1,2,0:T(8,128)(2,1)}, u32[]{:S(2)}, u32[]{:S(2)}) async-start(bf16[4,1024,256]{1,2,0:T(8,128)(2,1)} %stack.21), calls=%async_computation | async-start | bytes 4194304 | tf_op jit(solution)/shard_map/all_to_all | solution.py:9
  47.2 10.6 %collective-permute-start = (f32[2,1,128,256]{3,2,1,0:T(8,128)S(1)}, f32[2,1,128,256]{3,2,1,0:T(8,128)S(1)}, u32[]{:S(2)}, u32[]{:S(2)}) collective-permute-start(f32[2,1,128,256]{3,2,1,0:T(8,128)S(1)} %get-tuple-element.6), channel_id=1, source_target_pairs={{4,0},{8,4},{12,8},{16,12},{20,16},{24,20},{28,24},{32,28},{36,32}... | collective-permute-start | bytes 786440 | tf_op jit(solution)/shard_map/ppermute | solution.py:22
  57.8 1.9 %collective-permute-start.1 = (f32[2,1,128,256]{3,2,1,0:T(8,128)S(1)}, f32[2,1,128,256]{3,2,1,0:T(8,128)S(1)}, u32[]{:S(2)}, u32[]{:S(2)}) collective-permute-start(f32[2,1,128,256]{3,2,1,0:T(8,128)S(1)} %get-tuple-element.7), channel_id=1, source_target_pairs={{0,4},{4,8},{8,12},{12,16},{16,20},{20,24},{24,28},{28,32},{32,36}... | collective-permute-start | bytes 786440 | tf_op jit(solution)/shard_map/ppermute | solution.py:20
  60.3 2.1 %fusion.54 = (f32[8,127,256]{2,1,0:T(8,128)}, f32[8,127,256]{2,1,0:T(8,128)}, f32[8,127,256]{2,1,0:T(8,128)}, f32[8,127,256]{2,1,0:T(8,128)}) fusion(f32[8,128,256]{2,1,0:T(8,128)S(1)} %copy-done.1, f32[8,128,256]{2,1,0:T(8,128)S(1)} %copy-done), kind=kLoop, calls=%fused_computation.76 | loop fusion | bytes 8323072 | tf_op jit(solution)/shard_map/jit(_roll_static)/slice | solution.py:48
  62.4 3.2 %convolution_convert_fusion.2 = bf16[1024,256]{1,0:T(8,128)(2,1)} fusion(bf16[1024,1024]{0,1:T(8,128)(2,1)} %bitcast.14, bf16[2,1024,256]{2,1,0:T(8,128)(2,1)S(1)} %copy-done.21), kind=kOutput, calls=%fused_computation.2 | convolution fusion | flops 537133056 | bytes 3145728 | tf_op jit(solution)/shard_map/dot_general | solution.py:38
  65.6 3.1 %convolution_convert_fusion.3 = bf16[1024,256]{1,0:T(8,128)(2,1)} fusion(bf16[1024,1024]{0,1:T(8,128)(2,1)} %bitcast.14, bf16[2,1024,256]{2,1,0:T(8,128)(2,1)S(1)} %copy-done.21), kind=kOutput, calls=%fused_computation.3 | convolution fusion | flops 537133056 | bytes 3145728 | tf_op jit(solution)/shard_map/dot_general | solution.py:37
  68.8 8.9 %all-to-all-done = bf16[4,1024,256]{1,2,0:T(8,128)(2,1)} async-done(((bf16[4,1024,256]{1,2,0:T(8,128)(2,1)}), bf16[4,1024,256]{1,2,0:T(8,128)(2,1)}, u32[]{:S(2)}, u32[]{:S(2)}) %all-to-all-start) | async-done | bytes 2097184 | tf_op jit(solution)/shard_map/all_to_all | solution.py:9
  77.7 2.5 %convolution_convert_fusion.4 = bf16[1024,256]{1,0:T(8,128)(2,1)S(1)} fusion(bf16[1024,1024]{0,1:T(8,128)(2,1)} %bitcast.5, bf16[2,1024,256]{2,1,0:T(8,128)(2,1)} %param.9), kind=kOutput, calls=%fused_computation.4 | convolution fusion | flops 537133056 | bytes 3145728 | tf_op jit(solution)/shard_map/dot_general | solution.py:38
  80.3 2.5 %convolution_convert_fusion.5 = bf16[1024,256]{1,0:T(8,128)(2,1)S(1)} fusion(bf16[1024,1024]{0,1:T(8,128)(2,1)} %bitcast.5, bf16[2,1024,256]{2,1,0:T(8,128)(2,1)S(1)} %copy-done.22), kind=kOutput, calls=%fused_computation.5 | convolution fusion | flops 537133056 | bytes 3145728 | tf_op jit(solution)/shard_map/dot_general | solution.py:37
  83.6 3.5 %fusion.47 = (bf16[8,128,256]{2,1,0:T(8,128)(2,1)}, f32[8,128,256]{2,1,0:T(8,128)S(1)}, f32[8,128,256]{2,1,0:T(8,128)}, f32[8,128,256]{2,1,0:T(8,128)}) fusion(f32[256]{0:T(256)S(1)} %get-tuple-element.23, f32[8,128,256]{2,1,0:T(8,128)S(1)} %copy-done, f32[256]{0:T(256)S(1)} %copy-done.15, f32[8,128,256]{2,1,0:T(8,128)S(1)} %copy-done.11, ...), kind=kLoop, calls=%fused_computation.71 | loop fusion | flops 13369344 | bytes 15732736 | tf_op jit(solution)/shard_map/convert_element_type | solution.py:35
  87.2 2.4 %copy.10 = bf16[1024,256]{0,1:T(8,128)(2,1)} copy(bf16[1024,256]{1,0:T(8,128)(2,1)} %bitcast.86) | data formatting | bytes 1048576 | tf_op jit(solution)/shard_map/stack;reshape | solution.py:9
  89.6 2.7 %stack.23 = bf16[4,1024,256]{1,2,0:T(8,128)(2,1)} broadcast(bf16[1024,256]{0,1:T(8,128)(2,1)} %copy.10), dimensions={1,2} | broadcast | bytes 2621440 | tf_op jit(solution)/shard_map/stack | solution.py:9
  92.2 5.3 %all-to-all-start.2 = ((bf16[4,1024,256]{1,2,0:T(8,128)(2,1)}), bf16[4,1024,256]{1,2,0:T(8,128)(2,1)}, u32[]{:S(2)}, u32[]{:S(2)}) async-start(bf16[4,1024,256]{1,2,0:T(8,128)(2,1)} %stack.23), calls=%async_computation.2 | async-start | bytes 4194304 | tf_op jit(solution)/shard_map/all_to_all | solution.py:9
  98.2 10.6 %collective-permute-start.2 = (f32[1,128,256]{2,1,0:T(8,128)}, f32[1,128,256]{2,1,0:T(8,128)S(1)}, u32[]{:S(2)}, u32[]{:S(2)}) collective-permute-start(f32[1,128,256]{2,1,0:T(8,128)} %get-tuple-element.12), channel_id=1, source_target_pairs={{4,0},{8,4},{12,8},{16,12},{20,16},{24,20},{28,24},{32,28},{36,32}... | collective-permute-start | bytes 393224 | tf_op jit(solution)/shard_map/ppermute | solution.py:22
  108.7 1.9 %collective-permute-start.3 = (f32[1,128,256]{2,1,0:T(8,128)S(1)}, f32[1,128,256]{2,1,0:T(8,128)S(1)}, u32[]{:S(2)}, u32[]{:S(2)}) collective-permute-start(f32[1,128,256]{2,1,0:T(8,128)S(1)} %get-tuple-element.13), channel_id=1, source_target_pairs={{0,4},{4,8},{8,12},{12,16},{16,20},{20,24},{24,28},{28,32},{32,36}... | collective-permute-start | bytes 393224 | tf_op jit(solution)/shard_map/ppermute | solution.py:20
  110.7 1.5 %fusion.50 = (f32[8,127,256]{2,1,0:T(8,128)}, f32[8,127,256]{2,1,0:T(8,128)}) fusion(f32[8,128,256]{2,1,0:T(8,128)S(1)} %get-tuple-element.3), kind=kLoop, calls=%fused_computation.72 | loop fusion | bytes 4161536 | tf_op jit(solution)/shard_map/jit(_roll_static)/slice | solution.py:48
  112.2 13.1 %all-to-all-done.2 = bf16[4,1024,256]{1,2,0:T(8,128)(2,1)} async-done(((bf16[4,1024,256]{1,2,0:T(8,128)(2,1)}), bf16[4,1024,256]{1,2,0:T(8,128)(2,1)}, u32[]{:S(2)}, u32[]{:S(2)}) %all-to-all-start.2) | async-done | bytes 2097184 | tf_op jit(solution)/shard_map/all_to_all | solution.py:9
  125.3 2.5 %convolution_convert_fusion = bf16[1024,256]{1,0:T(8,128)(2,1)S(1)} fusion(bf16[1024,1024]{0,1:T(8,128)(2,1)} %bitcast.20, bf16[2,1024,256]{2,1,0:T(8,128)(2,1)} %param.9), kind=kOutput, calls=%fused_computation | convolution fusion | flops 537133056 | bytes 3145728 | tf_op jit(solution)/shard_map/dot_general | solution.py:38
  127.9 2.5 %convolution_convert_fusion.1 = bf16[1024,256]{1,0:T(8,128)(2,1)S(1)} fusion(bf16[1024,1024]{0,1:T(8,128)(2,1)} %bitcast.20, bf16[2,1024,256]{2,1,0:T(8,128)(2,1)S(1)} %copy-done.23), kind=kOutput, calls=%fused_computation.1 | convolution fusion | flops 537133056 | bytes 3145728 | tf_op jit(solution)/shard_map/dot_general | solution.py:37
  130.6 2.0 %fusion.13 = f32[8,128,256]{2,1,0:T(8,128)} fusion(f32[8,128,256]{2,1,0:T(8,128)S(1)} %get-tuple-element.3, f32[8,128,256]{2,1,0:T(8,128)S(1)} %copy-done.3, f32[1,128,256]{2,1,0:T(8,128)S(1)} %collective-permute-done.3, f32[1,128,256]{2,1,0:T(8,128)S(1)} %collective-permute-done.2, f32[8,127,256]{2,1,0:T(8,128)S(1)} %copy-done.6, ...), kind=kLoop, calls=%fused_computation.20 | loop fusion | flops 7340032 | bytes 9703424 | tf_op jit(solution)/shard_map/div | solution.py:65
  (61 shorter events, 4.1 us)
Async XLA Ops:
  3.7 11.4 %copy-start = (f32[8,128,256]{2,1,0:T(8,128)S(1)}, f32[8,128,256]{2,1,0:T(8,128)}, u32[]{:S(2)}) copy-start(f32[8,128,256]{2,1,0:T(8,128)} %param.7) | copy-start | bytes 3145732
  3.7 36.3 %all-to-all-start.1 = ((bf16[4,1024,256]{1,2,0:T(8,128)(2,1)}), bf16[4,1024,256]{1,2,0:T(8,128)(2,1)}, u32[]{:S(2)}, u32[]{:S(2)}) async-start(bf16[4,1024,256]{1,2,0:T(8,128)(2,1)} %stack.22), calls=%async_computation.1 | async-start | bytes 4194304 | tf_op jit(solution)/shard_map/all_to_all | solution.py:9
  41.7 5.4 %copy-start.1 = (f32[8,128,256]{2,1,0:T(8,128)S(1)}, f32[8,128,256]{2,1,0:T(8,128)}, u32[]{:S(2)}) copy-start(f32[8,128,256]{2,1,0:T(8,128)} %param.8) | copy-start | bytes 3145732
  41.7 36.0 %all-to-all-start = ((bf16[4,1024,256]{1,2,0:T(8,128)(2,1)}), bf16[4,1024,256]{1,2,0:T(8,128)(2,1)}, u32[]{:S(2)}, u32[]{:S(2)}) async-start(bf16[4,1024,256]{1,2,0:T(8,128)(2,1)} %stack.21), calls=%async_computation | async-start | bytes 4194304 | tf_op jit(solution)/shard_map/all_to_all | solution.py:9
  47.1 12.6 %copy-start.15 = (f32[256]{0:T(256)S(1)}, f32[256]{0:T(256)}, u32[]{:S(2)}) copy-start(f32[256]{0:T(256)} %param.11) | copy-start | bytes 3076
  47.2 35.6 %collective-permute-start = (f32[2,1,128,256]{3,2,1,0:T(8,128)S(1)}, f32[2,1,128,256]{3,2,1,0:T(8,128)S(1)}, u32[]{:S(2)}, u32[]{:S(2)}) collective-permute-start(f32[2,1,128,256]{3,2,1,0:T(8,128)S(1)} %get-tuple-element.6), channel_id=1, source_target_pairs={{4,0},{8,4},{12,8},{16,12},{20,16},{24,20},{28,24},{32,28},{36,32}... | collective-permute-start | bytes 786440 | tf_op jit(solution)/shard_map/ppermute | solution.py:22
  57.8 25.1 %collective-permute-start.1 = (f32[2,1,128,256]{3,2,1,0:T(8,128)S(1)}, f32[2,1,128,256]{3,2,1,0:T(8,128)S(1)}, u32[]{:S(2)}, u32[]{:S(2)}) collective-permute-start(f32[2,1,128,256]{3,2,1,0:T(8,128)S(1)} %get-tuple-element.7), channel_id=1, source_target_pairs={{0,4},{4,8},{8,12},{12,16},{16,20},{20,24},{24,28},{28,32},{32,36}... | collective-permute-start | bytes 786440 | tf_op jit(solution)/shard_map/ppermute | solution.py:20
  80.2 3.3 %copy-start.7 = (f32[8,127,256]{2,1,0:T(8,128)S(1)}, f32[8,127,256]{2,1,0:T(8,128)}, u32[]{:S(2)}) copy-start(f32[8,127,256]{2,1,0:T(8,128)} %get-tuple-element.16) | copy-start | bytes 3121156
  80.2 3.3 %copy-start.8 = (f32[8,127,256]{2,1,0:T(8,128)S(1)}, f32[8,127,256]{2,1,0:T(8,128)}, u32[]{:S(2)}) copy-start(f32[8,127,256]{2,1,0:T(8,128)} %get-tuple-element.17) | copy-start | bytes 3121156
  80.3 3.3 %copy-start.9 = (f32[8,127,256]{2,1,0:T(8,128)S(1)}, f32[8,127,256]{2,1,0:T(8,128)}, u32[]{:S(2)}) copy-start(f32[8,127,256]{2,1,0:T(8,128)} %get-tuple-element.28) | copy-start | bytes 3121156
  80.3 3.3 %copy-start.10 = (f32[8,127,256]{2,1,0:T(8,128)S(1)}, f32[8,127,256]{2,1,0:T(8,128)}, u32[]{:S(2)}) copy-start(f32[8,127,256]{2,1,0:T(8,128)} %get-tuple-element.29) | copy-start | bytes 3121156
  80.3 3.3 %copy-start.11 = (f32[8,128,256]{2,1,0:T(8,128)S(1)}, f32[8,128,256]{2,1,0:T(8,128)}, u32[]{:S(2)}) copy-start(f32[8,128,256]{2,1,0:T(8,128)} %param.6) | copy-start | bytes 3145732
  80.3 3.3 %copy-start.12 = (bf16[1024,256]{1,0:T(8,128)(2,1)S(1)}, bf16[1024,256]{1,0:T(8,128)(2,1)}, u32[]{:S(2)}) copy-start(bf16[1024,256]{1,0:T(8,128)(2,1)} %convolution_convert_fusion.2) | copy-start | bytes 1572868
  80.3 3.3 %copy-start.13 = (bf16[1024,256]{1,0:T(8,128)(2,1)S(1)}, bf16[1024,256]{1,0:T(8,128)(2,1)}, u32[]{:S(2)}) copy-start(bf16[1024,256]{1,0:T(8,128)(2,1)} %convolution_convert_fusion.3) | copy-start | bytes 1572868
  80.3 3.3 %copy-start.17 = (f32[256]{0:T(256)S(1)}, f32[256]{0:T(256)}, u32[]{:S(2)}) copy-start(f32[256]{0:T(256)} %param.10) | copy-start | bytes 3076
  87.2 43.2 %copy-start.2 = (f32[8,128,256]{2,1,0:T(8,128)}, f32[8,128,256]{2,1,0:T(8,128)S(1)}, u32[]{:S(2)}) copy-start(f32[8,128,256]{2,1,0:T(8,128)S(1)} %get-tuple-element.3) | copy-start | bytes 3145732
  92.2 33.0 %all-to-all-start.2 = ((bf16[4,1024,256]{1,2,0:T(8,128)(2,1)}), bf16[4,1024,256]{1,2,0:T(8,128)(2,1)}, u32[]{:S(2)}, u32[]{:S(2)}) async-start(bf16[4,1024,256]{1,2,0:T(8,128)(2,1)} %stack.23), calls=%async_computation.2 | async-start | bytes 4194304 | tf_op jit(solution)/shard_map/all_to_all | solution.py:9
  98.2 32.2 %collective-permute-start.2 = (f32[1,128,256]{2,1,0:T(8,128)}, f32[1,128,256]{2,1,0:T(8,128)S(1)}, u32[]{:S(2)}, u32[]{:S(2)}) collective-permute-start(f32[1,128,256]{2,1,0:T(8,128)} %get-tuple-element.12), channel_id=1, source_target_pairs={{4,0},{8,4},{12,8},{16,12},{20,16},{24,20},{28,24},{32,28},{36,32}... | collective-permute-start | bytes 393224 | tf_op jit(solution)/shard_map/ppermute | solution.py:22
  108.7 21.6 %collective-permute-start.3 = (f32[1,128,256]{2,1,0:T(8,128)S(1)}, f32[1,128,256]{2,1,0:T(8,128)S(1)}, u32[]{:S(2)}, u32[]{:S(2)}) collective-permute-start(f32[1,128,256]{2,1,0:T(8,128)S(1)} %get-tuple-element.13), channel_id=1, source_target_pairs={{0,4},{4,8},{8,12},{12,16},{16,20},{20,24},{24,28},{28,32},{32,36}... | collective-permute-start | bytes 393224 | tf_op jit(solution)/shard_map/ppermute | solution.py:20
  127.8 2.8 %copy-start.6 = (f32[8,127,256]{2,1,0:T(8,128)S(1)}, f32[8,127,256]{2,1,0:T(8,128)}, u32[]{:S(2)}) copy-start(f32[8,127,256]{2,1,0:T(8,128)} %get-tuple-element.9) | copy-start | bytes 3121156
  127.8 2.8 %copy-start.16 = (f32[256]{0:T(256)S(1)}, f32[256]{0:T(256)}, u32[]{:S(2)}) copy-start(f32[256]{0:T(256)} %param.11) | copy-start | bytes 3076
  127.8 2.8 %copy-start.18 = (f32[256]{0:T(256)S(1)}, f32[256]{0:T(256)}, u32[]{:S(2)}) copy-start(f32[256]{0:T(256)} %param.10) | copy-start | bytes 3076
  127.9 2.8 %copy-start.19 = (f32[256]{0:T(256)S(1)}, f32[256]{0:T(256)}, u32[]{:S(2)}) copy-start(f32[256]{0:T(256)} %get-tuple-element.22) | copy-start | bytes 3076
  127.9 2.7 %copy-start.20 = (f32[256]{0:T(256)S(1)}, f32[256]{0:T(256)}, u32[]{:S(2)}) copy-start(f32[256]{0:T(256)} %get-tuple-element.24) | copy-start | bytes 3076
  (7 other events, 15.8 us)
